TPU v7x, 256 devices: a whole 4x4x8 slice. The times are simulated.
256 devices in a mesh: gx: 8 (over x, core), gy: 32 (over y, z).
Axes of the slice: x: 4, y: 4, z: 8, core: 2. Of those that a mesh axis runs over, the one named last changes fastest.
Arguments:
- features: float32 [64, 524288], P(None, ('gx', 'gy')), may hold values from -6 to 6
- cotangent: float32 [64, 524288], P(None, ('gx', 'gy')), may hold values from -6 to 6
- edge_src: int32 [8, 524288], P(None, ('gx', 'gy')), may hold values from 0 to 2559
- send_rows: int32 [4, 32768], P(None, ('gx', 'gy')), may hold values from 0 to 2047
- fine_to_coarse: int32 [524288], P(('gx', 'gy')), may hold values from 0 to 2047
- coarse_to_fine: int32 [524288], P(('gx', 'gy')), may hold values from 0 to 2047
- coarse_edges: int32 [2, 8192], replicated, may hold values from 0 to 2047
- edge_in: float32 [64, 128], replicated, may hold values from -0.5 to 0.5
- edge_out: float32 [64, 64], replicated, may hold values from -0.75 to 0.75
- node_in: float32 [64, 128], replicated, may hold values from -0.5 to 0.5
- node_out: float32 [64, 64], replicated, may hold values from -0.75 to 0.75
- coarse_in: float32 [64, 64], replicated, may hold values from -0.75 to 0.75
- coarse_out: float32 [64, 64], replicated, may hold values from -0.75 to 0.75
- coarse_mix: float32 [64, 64], replicated, may hold values from -0.75 to 0.75
- up_in: float32 [64, 128], replicated, may hold values from -0.5 to 0.5
- up_out: float32 [64, 64], replicated, may hold values from -0.75 to 0.75
- biases: float32 [4, 64], replicated, may hold values from -3 to 3
Outputs:
- output: float32 [64, 524288], P(None, ('gx', 'gy'))
- grad_features: float32 [64, 524288], P(None, ('gx', 'gy'))
- grad_edge_in: float32 [64, 128], replicated
- grad_edge_out: float32 [64, 64], replicated
- grad_node_in: float32 [64, 128], replicated
- grad_node_out: float32 [64, 64], replicated
- grad_coarse_in: float32 [64, 64], replicated
- grad_coarse_out: float32 [64, 64], replicated
- grad_coarse_mix: float32 [64, 64], replicated
- grad_up_in: float32 [64, 128], replicated
- grad_up_out: float32 [64, 64], replicated
- grad_biases: float32 [4, 64], replicated
Inputs may be any that keep to these rules, and one draw needn't show every extreme that they name: `edge_src`: indexes the receiver partition's 2048 own nodes, then the four received packets in the order of the first step. `send_rows`: partition-local node numbers.
All inputs are finite; a program needn't handle non-finite values.
Results may differ from a plain program's by a relative error of at most 0.0003.
Values sent between devices are 32-bit elements; how exact they have to be, the bound alone decides.
A program may use at most 64 MiB of HBM per device.

v0:
```python
from functools import partial
import math
import jax
import jax.numpy as jnp
from jax import lax
from jax.sharding import PartitionSpec as P

COARSE = 2048


def passed_along(value, axis, steps):
    count = lax.axis_size(axis)
    leading, last = (max(0, -steps), min(count, count - steps))
    return lax.ppermute(value, axis, [(source, source + steps) for source in range(leading, last)])


def matmul(left_side, right_side):
    return jnp.dot(
        left_side, right_side, precision=lax.Precision.HIGHEST, preferred_element_type=jnp.float32
    )


def swish(values):
    return values * jax.nn.sigmoid(values)


def fine_update(
    latent, extended, edge_in, edge_out, node_in, node_out, edge_bias, node_bias, sources
):
    feature_count = latent.shape[0]
    receiver_part = matmul(edge_in[:, :feature_count], latent)
    sender_part = matmul(edge_in[:, feature_count:], extended)
    hidden = swish(receiver_part[:, None, :] + sender_part[:, sources] + edge_bias[:, None, None])
    summed = matmul(edge_out, jnp.sum(hidden, axis=1))
    activation = swish(
        matmul(node_in[:, :feature_count], latent)
        + matmul(node_in[:, feature_count:], summed)
        + node_bias[:, None]
    )
    return latent + matmul(node_out, activation)


def coarse_node(pooled, coarse_in, coarse_out, coarse_bias):
    return pooled + matmul(coarse_out, swish(matmul(coarse_in, pooled) + coarse_bias[:, None]))


def coarse_edge(nodes, coarse_mix, coarse_edges):
    gathered = nodes[:, coarse_edges[0]]
    summed = jnp.zeros_like(nodes).at[:, coarse_edges[1]].add(gathered)
    factor = (nodes.shape[1] / coarse_edges.shape[1]) ** 0.5
    return nodes + matmul(coarse_mix, summed) * factor


def up_update(middle, looked, up_in, up_out, up_bias):
    feature_count = middle.shape[0]
    activation = swish(
        matmul(up_in[:, :feature_count], middle)
        + matmul(up_in[:, feature_count:], looked)
        + up_bias[:, None]
    )
    return middle + matmul(up_out, activation)


def block_width(node_count):
    return math.gcd(node_count, 1024)


def one_hot_block(index_block, table_width):
    return (index_block[:, None] == jnp.arange(table_width, dtype=jnp.int32)[None, :]).astype(
        jnp.float32
    )


def pool_nodes(values, index, table_width):
    feature_count, node_count = values.shape
    width = block_width(node_count)
    blocks = node_count // width
    value_blocks = values.reshape(feature_count, blocks, width).transpose(1, 0, 2)
    index_blocks = index.reshape(blocks, width)

    def add_block(total, items):
        return (total + matmul(items[0], one_hot_block(items[1], table_width)), None)

    start = jnp.zeros((feature_count, table_width), jnp.float32)
    total, unused = lax.scan(add_block, start, (value_blocks, index_blocks))
    return total


def look_nodes(table, index):
    feature_count, table_width = table.shape
    node_count = index.shape[0]
    width = block_width(node_count)
    blocks = node_count // width
    index_blocks = index.reshape(blocks, width)

    def read_block(index_block):
        selector = one_hot_block(index_block, table_width)
        return lax.dot_general(
            table,
            selector,
            (((1,), (1,)), ((), ())),
            precision=lax.Precision.HIGHEST,
            preferred_element_type=jnp.float32,
        )

    result = lax.map(read_block, index_blocks)
    return result.transpose(1, 0, 2).reshape(feature_count, node_count)


def pass_rows(packet, offset):
    return passed_along(packet, "gx", offset)


def pass_cols(packet, offset):
    return passed_along(packet, "gy", offset)


def coarse_total(table):
    return lax.psum(table, ("gx", "gy"))


def local(
    features,
    cotangent,
    edge_src,
    send_rows,
    fine_to_coarse,
    coarse_to_fine,
    coarse_edges,
    edge_in,
    edge_out,
    node_in,
    node_out,
    coarse_in,
    coarse_out,
    coarse_mix,
    up_in,
    up_out,
    biases,
):
    local_nodes = features.shape[1]
    halo_rows = send_rows.shape[1]
    pool_scale = (COARSE / (local_nodes * lax.axis_size("gx") * lax.axis_size("gy"))) ** 0.5
    packets = features[:, send_rows]
    extended = jnp.concatenate(
        [
            features,
            pass_rows(packets[:, 0], 1),
            pass_rows(packets[:, 1], -1),
            pass_cols(packets[:, 2], 1),
            pass_cols(packets[:, 3], -1),
        ],
        axis=1,
    )
    middle, fine_back = jax.vjp(
        partial(fine_update, sources=edge_src),
        features,
        extended,
        edge_in,
        edge_out,
        node_in,
        node_out,
        biases[0],
        biases[1],
    )
    pooled_part = pool_nodes(middle, fine_to_coarse, COARSE) * pool_scale
    pooled = coarse_total(pooled_part)
    nodes, node_back = jax.vjp(coarse_node, pooled, coarse_in, coarse_out, biases[2])
    mixed, mix_back = jax.vjp(partial(coarse_edge, coarse_edges=coarse_edges), nodes, coarse_mix)
    looked = look_nodes(mixed, coarse_to_fine)
    output, up_back = jax.vjp(up_update, middle, looked, up_in, up_out, biases[3])
    grad_middle, grad_looked, grad_up_in, grad_up_out, grad_up_bias = up_back(cotangent)
    grad_mixed_part = pool_nodes(grad_looked, coarse_to_fine, COARSE)
    grad_nodes_part, grad_mix = mix_back(grad_mixed_part)
    grad_nodes = coarse_total(grad_nodes_part)
    grad_pooled, grad_coarse_in, grad_coarse_out, grad_coarse_bias = node_back(grad_nodes)
    grad_middle = grad_middle + look_nodes(grad_pooled, fine_to_coarse) * pool_scale
    (
        grad_own,
        grad_ext,
        grad_edge_in,
        grad_edge_out,
        grad_node_in,
        grad_node_out,
        grad_edge_bias,
        grad_node_bias,
    ) = fine_back(grad_middle)
    pieces = [
        grad_ext[:, local_nodes + slot * halo_rows : local_nodes + (slot + 1) * halo_rows]
        for slot in range(4)
    ]
    returned = jnp.stack(
        [
            pass_rows(pieces[0], -1),
            pass_rows(pieces[1], 1),
            pass_cols(pieces[2], -1),
            pass_cols(pieces[3], 1),
        ],
        axis=1,
    )
    grad_features = (
        grad_own
        + grad_ext[:, :local_nodes]
        + jnp.zeros_like(features).at[:, send_rows].add(returned)
    )
    fine_biases = jnp.stack([grad_edge_bias, grad_node_bias, grad_up_bias])
    summed = lax.psum(
        (
            grad_edge_in,
            grad_edge_out,
            grad_node_in,
            grad_node_out,
            grad_mix,
            grad_up_in,
            grad_up_out,
            fine_biases,
        ),
        ("gx", "gy"),
    )
    grad_biases = jnp.stack([summed[7][0], summed[7][1], grad_coarse_bias, summed[7][2]])
    return (
        output,
        grad_features,
        summed[0],
        summed[1],
        summed[2],
        summed[3],
        grad_coarse_in,
        grad_coarse_out,
        summed[4],
        summed[5],
        summed[6],
        grad_biases,
    )


def solution(mesh):
    in_specs = (
        P(None, ("gx", "gy")),
        P(None, ("gx", "gy")),
        P(None, ("gx", "gy")),
        P(None, ("gx", "gy")),
        P(("gx", "gy")),
        P(("gx", "gy")),
        P(),
        P(),
        P(),
        P(),
        P(),
        P(),
        P(),
        P(),
        P(),
        P(),
        P(),
    )
    out_specs = (
        P(None, ("gx", "gy")),
        P(None, ("gx", "gy")),
        P(),
        P(),
        P(),
        P(),
        P(),
        P(),
        P(),
        P(),
        P(),
        P(),
    )
    return jax.shard_map(local, mesh=mesh, in_specs=in_specs, out_specs=out_specs, check_vma=False)
```

profile of v0, /device:TPU:4, one launch (start us, length us, event | category | flops | bytes accessed | tf_op | source)
XLA Modules:
  0.0 1284.9 jit_solution(6008554091809120378)
XLA Ops:
  11.8 4.5 collective-permute-start.2
  16.3 1.9 collective-permute-start.1
  18.3 2.4 collective-permute-start
  24.3 2.9 fusion.81
  27.2 2.9 fusion.102
  34.0 1.5 convolution_bitcast_fusion.1
  35.8 54.7 %gather_fusion.1 = f32[16384,64]{1,0:T(8,128)} fusion(f32[64,2560]{0,1:T(8,128)S(1)} %copy.65, s32[16384]{0:T(1024)S(1)} %broadcast_clamp_fusion), kind=kCustom, calls=%fused_computation.1 | custom fusion | bytes 8454144 | tf_op jit(solution)/shard_map/jvp()/gather | solution.py:33
  90.6 4.8 multiply_reduce_fusion
  100.4 7.0 while.44
  100.5 3.5 fusion.178
  104.0 3.5 fusion.178
  108.7 1.4 fusion.73
  110.1 254.7 %all-reduce.11.cloned.1.call-done = f32[64,2048]{1,0:T(8,128)} async-done(((f32[64,2048]{1,0:T(8,128)}), f32[64,2048]{1,0:T(8,128)}) %all-reduce.11.cloned.1.call-update) | async-done | bytes 524304 | tf_op jit(solution)/shard_map/psum | solution.py:119
  364.8 1.6 fusion.40
  367.3 1.8 fusion.38
  370.4 90.5 %scatter_custom_fusion = f32[64,2048]{0,1:T(8,128)S(1)} fusion(s32[8192]{0:T(1024)} %bitcast.245, f32[64,2048]{0,1:T(8,128)} %copy.67, s32[8192]{0:T(1024)} %broadcast_clamp_fusion.2, f32[]{:T(128)} %constant.19.clone.1), kind=kCustom, calls=%fused_computation.44 | custom fusion | flops 524288 | bytes 524800 | tf_op jit(solution)/shard_map/jvp()/scatter-add | solution.py:49
  460.9 2.1 fusion.29
  463.0 11.0 while.42
  463.1 5.5 fusion.174
  468.6 5.5 fusion.174
  474.1 2.2 fusion.96
  476.3 2.3 convolution_bitcast_fusion.14
  478.6 2.6 fusion.37
  485.0 10.4 while.45
  485.0 5.1 fusion.180
  490.1 5.3 fusion.180
  495.4 2.5 convolution_bitcast_fusion.7
  497.9 2.4 copy.71
  500.2 2.4 copy.70
  502.6 103.6 %scatter_custom_fusion.1 = f32[64,2048]{0,1:T(8,128)} fusion(f32[64,2048]{0,1:T(8,128)} %copy.71, s32[8192]{0:T(1024)} %bitcast.243, f32[]{:T(128)} %constant.19.clone.1, pred[8192]{0:T(1024)(128)(4,1)S(1)} %compare_and_fusion, f32[64,2048]{0,1:T(8,128)} %copy.70, s32[8192]{0:T(1024)S(1)} %broadcast_clamp_fusion.1), kind=kCustom, calls=%fused_computation.42 | custom fusion | flops 1048576 | bytes 1614336 | tf_op jit(solution)/shard_map/transpose(jvp())/scatter-add | solution.py:48
  606.2 2.3 copy.72
  608.6 2.4 fusion.55
  611.0 248.5 %all-reduce.13.cloned.1.call-done = f32[64,2048]{1,0:T(8,128)} async-done(((f32[64,2048]{1,0:T(8,128)}), f32[64,2048]{1,0:T(8,128)}) %all-reduce.13.cloned.1.call-update) | async-done | bytes 524304 | tf_op jit(solution)/shard_map/psum | solution.py:119
  859.5 2.6 fusion.100
  862.9 1.7 fusion.34
  864.6 8.9 while.43
  864.6 4.4 fusion.176
  869.1 4.4 fusion.176
  875.6 1.7 fusion.36
  877.3 2.6 fusion.62
  879.9 1.9 fusion.99
  886.2 1.4 convolution_bitcast_fusion.2
  889.0 5.7 fusion.21
  894.7 3.2 copy-done.1
  898.0 2.5 fusion.95
  900.4 2.5 fusion.104
  902.9 2.1 convolution_bitcast_fusion.13
  905.0 88.0 %scatter_custom_fusion.2 = f32[64,2560]{0,1:T(8,128)S(1)} fusion(s32[16384]{0:T(1024)S(1)} %bitcast.240, f32[16384,64]{1,0:T(8,128)} %bitcast.227, f32[]{:T(128)} %constant.19.clone.1), kind=kCustom, calls=%fused_computation.85 | custom fusion | flops 1048576 | bytes 655872 | tf_op jit(solution)/shard_map/transpose(jvp())/scatter-add | solution.py:33
  993.0 2.2 fusion.103
  995.2 1.6 convolution_bitcast_fusion
  996.8 1.8 fusion.33
  998.7 1.9 collective-permute-start.4
  1000.6 1.9 collective-permute-start.7
  1003.8 2.2 collective-permute-start.5
  1006.0 1.5 pad_add_fusion.2
  1008.1 1.5 pad_add_fusion
  1009.6 2.5 fusion.65
  1012.1 2.4 fusion.108
  1015.1 3.7 scatter_fusion
  1019.9 246.4 %all-reduce.15.cloned.1.call-done = (f32[64,128]{1,0:T(8,128)}, f32[64,64]{1,0:T(8,128)}, f32[64,128]{1,0:T(8,128)}, f32[64,64]{1,0:T(8,128)}, f32[64,64]{1,0:T(...) async-done(((f32[64,128]{1,0:T(8,128)}, f32[64,64]{1,0:T(8,128)}, f32[64,128]{1,0:T(8,128)}, f32[64,64]{1,0:T(8,128)}, f32[64,64]{1,0:T(8,128)}, ...) | async-done | bytes 164624 | tf_op jit(solution)/shard_map/psum | solution.py:207
  1267.6 1.5 copy.79
  1269.7 1.4 copy.139
  1272.4 1.4 copy.141
  1275.2 1.4 copy.143
  (143 shorter events, 42.9 us)
Async XLA Ops:
  7.2 360.1 %copy-start = (f32[64,64]{1,0:T(8,128)S(1)}, f32[64,64]{1,0:T(8,128)}, u32[]{:S(2)}) copy-start(f32[64,64]{1,0:T(8,128)} %param.37) | copy-start | bytes 49156
  7.2 357.6 %all-reduce.11.cloned.1.call-start = ((), (), s32[]{:S(2)}) async-start(), calls=%async_computation | async-start | bytes 1048576 | tf_op jit(solution)/shard_map/psum | solution.py:119
  10.5 22.6 %collective-permute-start.3 = (f32[64,128]{1,0:T(8,128)S(1)}, f32[64,128]{1,0:T(8,128)S(1)}, u32[]{:S(2)}, u32[]{:S(2)}) collective-permute-start(f32[64,128]{1,0:T(8,128)S(1)} %get-tuple-element.218), channel_id=1, source_target_pairs={{1,0},{2,1},{3,2},{4,3},{5,4},{6,5},{7,6},{8,7},{9,8},{10,9},{11,1... | collective-permute-start | bytes 98312 | tf_op jit(solution)/shard_map/ppermute | solution.py:14
  11.8 21.3 %collective-permute-start.2 = (f32[64,128]{1,0:T(8,128)S(1)}, f32[64,128]{1,0:T(8,128)S(1)}, u32[]{:S(2)}, u32[]{:S(2)}) collective-permute-start(f32[64,128]{1,0:T(8,128)S(1)} %get-tuple-element.219), channel_id=1, source_target_pairs={{0,1},{1,2},{2,3},{3,4},{4,5},{5,6},{6,7},{7,8},{8,9},{9,10},{10,1... | collective-permute-start | bytes 98312 | tf_op jit(solution)/shard_map/ppermute | solution.py:14
  16.3 16.7 %collective-permute-start.1 = (f32[64,128]{1,0:T(8,128)S(1)}, f32[64,128]{1,0:T(8,128)S(1)}, u32[]{:S(2)}, u32[]{:S(2)}) collective-permute-start(f32[64,128]{1,0:T(8,128)S(1)} %get-tuple-element.220), channel_id=1, source_target_pairs={{32,0},{64,32},{96,64},{128,96},{160,128},{192,160},{224,192},{33,... | collective-permute-start | bytes 98312 | tf_op jit(solution)/shard_map/ppermute | solution.py:14
  18.3 14.7 %collective-permute-start = (f32[64,128]{1,0:T(8,128)S(1)}, f32[64,128]{1,0:T(8,128)S(1)}, u32[]{:S(2)}, u32[]{:S(2)}) collective-permute-start(f32[64,128]{1,0:T(8,128)S(1)} %get-tuple-element.221), channel_id=1, source_target_pairs={{0,32},{32,64},{64,96},{96,128},{128,160},{160,192},{192,224},{1,3... | collective-permute-start | bytes 98312 | tf_op jit(solution)/shard_map/ppermute | solution.py:14
  23.7 6.4 copy-start.24
  23.7 12.2 copy-start.23
  27.2 63.4 %copy-start.3 = (f32[64,2048]{0,1:T(8,128)}, f32[64,2048]{0,1:T(8,128)S(1)}, u32[]{:S(2)}) copy-start(f32[64,2048]{0,1:T(8,128)S(1)} %fusion.81) | copy-start | bytes 1572868
  33.1 0.9 copy-start.5
  90.6 4.9 copy-start.22
  90.6 7.0 copy-start.18
  90.6 7.6 copy-start.2
  90.6 9.0 copy-start.29
  90.6 9.8 copy-start.16
  96.8 0.8 copy-start.7
  98.8 0.8 copy-start.15
  100.3 8.3 copy-start.9
  100.4 8.2 copy-start.26
  100.4 8.3 copy-start.19
  100.4 264.3 %copy-start.21 = (f32[64,64]{1,0:T(8,128)S(1)}, f32[64,64]{1,0:T(8,128)}, u32[]{:S(2)}) copy-start(f32[64,64]{1,0:T(8,128)} %param.36) | copy-start | bytes 49156
  107.4 353.4 %copy-start.20 = (f32[64,64]{1,0:T(8,128)S(1)}, f32[64,64]{1,0:T(8,128)}, u32[]{:S(2)}) copy-start(f32[64,64]{1,0:T(8,128)} %param.38) | copy-start | bytes 49156
  108.3 751.2 %all-reduce.13.cloned.1.call-start = ((), (), s32[]{:S(2)}) async-start(), calls=%async_computation.1 | async-start | bytes 1048576 | tf_op jit(solution)/shard_map/psum | solution.py:119
  366.4 0.8 copy-start.17
  463.0 11.1 copy-start.28
  463.0 15.5 %copy-start.25 = (f32[64,64]{1,0:T(8,128)S(1)}, f32[64,64]{1,0:T(8,128)}, u32[]{:S(2)}) copy-start(f32[64,64]{1,0:T(8,128)} %param.40) | copy-start | bytes 49156
  474.0 8.3 copy-start.10
  608.5 657.8 %all-reduce.15.cloned.1.call-start = ((), (), s32[]{:S(2)}) async-start(), calls=%async_computation.2 | async-start | bytes 462848 | tf_op jit(solution)/shard_map/psum | solution.py:207
  862.1 0.8 copy-start.11
  864.6 15.3 %copy-start.30 = (f32[64,64]{1,0:T(8,128)S(1)}, f32[64,64]{1,0:T(8,128)}, u32[]{:S(2)}) copy-start(f32[64,64]{1,0:T(8,128)} %param.35) | copy-start | bytes 49156
  873.5 0.8 copy-start.12
  874.3 7.4 copy-start.8
  874.3 14.6 %copy-start.4 = (f32[64,2048]{0,1:T(8,128)S(1)}, f32[64,2048]{0,1:T(8,128)}, u32[]{:S(2)}) copy-start(f32[64,2048]{0,1:T(8,128)} %copy-done.3) | copy-start | bytes 1572868
  877.3 5.7 copy-start.13
  894.7 3.2 copy-start.1
  897.9 4.9 copy-start.14
  897.9 95.0 %copy-start.6 = (f32[64,2560]{1,0:T(8,128)S(1)}, f32[64,2560]{1,0:T(8,128)}, u32[]{:S(2)}) copy-start(f32[64,2560]{1,0:T(8,128)} %copy-done.5) | copy-start | bytes 1966084
  992.9 276.1 %copy-start.27 = (f32[64]{0:T(128)S(1)}, f32[64]{0:T(128)}, u32[]{:S(2)}) copy-start(f32[64]{0:T(128)} %get-tuple-element.231) | copy-start | bytes 772
  998.7 16.2 %collective-permute-start.4 = (f32[64,128]{1,0:T(8,128)S(1)}, f32[64,128]{1,0:T(8,128)S(1)}, u32[]{:S(2)}, u32[]{:S(2)}) collective-permute-start(f32[64,128]{1,0:T(8,128)S(1)} %get-tuple-element.214), channel_id=1, source_target_pairs={{32,0},{64,32},{96,64},{128,96},{160,128},{192,160},{224,192},{33,... | collective-permute-start | bytes 98312 | tf_op jit(solution)/shard_map/ppermute | solution.py:14
  1000.6 14.3 %collective-permute-start.7 = (f32[64,128]{1,0:T(8,128)S(1)}, f32[64,128]{1,0:T(8,128)S(1)}, u32[]{:S(2)}, u32[]{:S(2)}) collective-permute-start(f32[64,128]{1,0:T(8,128)S(1)} %get-tuple-element.215), channel_id=1, source_target_pairs={{0,1},{1,2},{2,3},{3,4},{4,5},{5,6},{6,7},{7,8},{8,9},{9,10},{10,1... | collective-permute-start | bytes 98312 | tf_op jit(solution)/shard_map/ppermute | solution.py:14
  1002.5 12.3 collective-permute-start.6
  1003.8 11.1 collective-permute-start.5
Sparse Core Ops, SparseCore 0:
  108.4 256.2 all-reduce.10
  608.6 250.7 all-reduce.12
  1009.7 256.5 all-reduce.14
where the time goes:
time: 1300 us; the launch traced here: 1280 us
  waiting for transfers between devices  750 us (58%)
  other arithmetic  308 us (24%)
  matrix products  101 us (8%)
  local copies, waits for them, and re-layouts  93.4 us (7%)
  starting transfers between devices  17.9 us (1%)
  between operations  15 us (1%)
    psum x2, waiting for transfers between devices, coarse_total(): return lax.psum(table, ('gx', 'gy'))  503 us
    psum x1, waiting for transfers between devices, local(): lax.psum((grad_edge_in, grad_edge_out, grad_node_in, grad_node_out, grad_...  246 us
    scatter-add x1, other arithmetic, coarse_edge(): gathered = nodes[:, coarse_edges[0]]  104 us
    scatter-add x1, other arithmetic, coarse_edge(): summed = jnp.zeros_like(nodes).at[:, coarse_edges[1]].add(gathered)  90.5 us
    scatter-add x1, other arithmetic, fine_update(): sender_part[:, sources]  88 us
    dot_general x40, matrix products, matmul(): jnp.dot(left_side, right_side, precision=lax.Precision.HIGHEST, preferred...  80.9 us
    gather x1, local copies, waits for them, and re-layouts, fine_update(): sender_part[:, sources]  54.7 us
  transfers between devices with their start and end apart: 11, of which 3 were waited for; matrix products, arithmetic and copies ran while one was open for 2% of the time, Pallas kernels for 0%

commit v1 on v0

--- a/solution.py
+++ b/solution.py
@@ -204,7 +204,7 @@
         + jnp.zeros_like(features).at[:, send_rows].add(returned)
     )
     fine_biases = jnp.stack([grad_edge_bias, grad_node_bias, grad_up_bias])
-    summed = lax.psum(
+    partial_2 = lax.psum(
         (
             grad_edge_in,
             grad_edge_out,
@@ -215,8 +215,9 @@
             grad_up_out,
             fine_biases,
         ),
-        ("gx", "gy"),
-    )
+        "gy",
+    )
+    summed = lax.psum(partial_2, "gx")
     grad_biases = jnp.stack([summed[7][0], summed[7][1], grad_coarse_bias, summed[7][2]])
     return (
         output,

time: 1300 us -> 1250 us (0.962)
  waiting for transfers between devices: 750 us -> 701 us
    psum x1, waiting for transfers between devices: 246 us -> 143 us  [local(): lax.psum((grad_edge_in, grad_edge_out, grad_node_in, grad_node_out, grad_...]
    psum x0 -> x1, waiting for transfers between devices: none -> 56.1 us  [local(): summed = lax.psum(partial_2, 'gx')]
  transfers between devices with their start and end apart: 11 -> 12, of which waited for: 3 -> 4; matrix products, arithmetic and copies ran while one was open for 2% -> 2% of each run, Pallas kernels for 0% -> 0%
where the time goes in v1:
time: 1250 us; the launch traced here: 1240 us
  waiting for transfers between devices  701 us (56%)
  other arithmetic  308 us (25%)
  matrix products  99.8 us (8%)
  local copies, waits for them, and re-layouts  93.5 us (7%)
  starting transfers between devices  17.9 us (1%)
  between operations  15 us (1%)
    psum x2, waiting for transfers between devices, coarse_total(): return lax.psum(table, ('gx', 'gy'))  503 us
    psum x1, waiting for transfers between devices, local(): lax.psum((grad_edge_in, grad_edge_out, grad_node_in, grad_node_out, grad_...  143 us
    scatter-add x1, other arithmetic, coarse_edge(): gathered = nodes[:, coarse_edges[0]]  104 us
    scatter-add x1, other arithmetic, coarse_edge(): summed = jnp.zeros_like(nodes).at[:, coarse_edges[1]].add(gathered)  90.4 us
    scatter-add x1, other arithmetic, fine_update(): sender_part[:, sources]  88 us
    dot_general x40, matrix products, matmul(): jnp.dot(left_side, right_side, precision=lax.Precision.HIGHEST, preferred...  80 us
    psum x1, waiting for transfers between devices, local(): summed = lax.psum(partial_2, 'gx')  56.1 us
    gather x1, local copies, waits for them, and re-layouts, fine_update(): sender_part[:, sources]  54.8 us
  transfers between devices with their start and end apart: 12, of which 4 were waited for; matrix products, arithmetic and copies ran while one was open for 2% of the time, Pallas kernels for 0%

profile of v1, /device:TPU:4, one launch (start us, length us, event | category | flops | bytes accessed | tf_op | source)
XLA Modules:
  0.0 1235.9 jit_solution(3382150932103333819)
XLA Ops:
  11.8 4.5 collective-permute-start.2
  16.3 1.9 collective-permute-start.1
  18.3 2.4 collective-permute-start
  24.3 2.9 fusion.81
  27.2 2.9 fusion.102
  33.9 1.5 convolution_bitcast_fusion.1
  35.8 54.8 %gather_fusion.1 = f32[16384,64]{1,0:T(8,128)} fusion(f32[64,2560]{0,1:T(8,128)S(1)} %copy.65, s32[16384]{0:T(1024)S(1)} %broadcast_clamp_fusion), kind=kCustom, calls=%fused_computation.1 | custom fusion | bytes 8454144 | tf_op jit(solution)/shard_map/jvp()/gather | solution.py:33
  90.6 4.8 multiply_reduce_fusion
  100.5 7.0 while.44
  100.5 3.5 fusion.178
  104.0 3.5 fusion.178
  108.7 1.4 fusion.73
  110.1 254.5 %all-reduce.13.cloned.1.call-done = f32[64,2048]{1,0:T(8,128)} async-done(((f32[64,2048]{1,0:T(8,128)}), f32[64,2048]{1,0:T(8,128)}) %all-reduce.13.cloned.1.call-update) | async-done | bytes 524304 | tf_op jit(solution)/shard_map/psum | solution.py:119
  364.6 1.6 fusion.40
  367.1 1.8 fusion.38
  370.3 90.4 %scatter_custom_fusion = f32[64,2048]{0,1:T(8,128)S(1)} fusion(s32[8192]{0:T(1024)} %bitcast.245, f32[64,2048]{0,1:T(8,128)} %copy.67, s32[8192]{0:T(1024)} %broadcast_clamp_fusion.2, f32[]{:T(128)} %constant.19.clone.1), kind=kCustom, calls=%fused_computation.44 | custom fusion | flops 524288 | bytes 524800 | tf_op jit(solution)/shard_map/jvp()/scatter-add | solution.py:49
  460.7 2.1 fusion.29
  462.9 11.0 while.42
  462.9 5.5 fusion.174
  468.4 5.5 fusion.174
  473.9 2.2 fusion.96
  476.1 2.3 convolution_bitcast_fusion.14
  478.4 2.6 fusion.37
  484.9 10.3 while.45
  484.9 5.1 fusion.180
  490.0 5.2 fusion.180
  495.2 2.5 convolution_bitcast_fusion.7
  497.7 2.4 copy.71
  500.1 2.4 copy.70
  502.4 103.6 %scatter_custom_fusion.1 = f32[64,2048]{0,1:T(8,128)} fusion(f32[64,2048]{0,1:T(8,128)} %copy.71, s32[8192]{0:T(1024)} %bitcast.243, f32[]{:T(128)} %constant.19.clone.1, pred[8192]{0:T(1024)(128)(4,1)S(1)} %compare_and_fusion, f32[64,2048]{0,1:T(8,128)} %copy.70, s32[8192]{0:T(1024)S(1)} %broadcast_clamp_fusion.1), kind=kCustom, calls=%fused_computation.42 | custom fusion | flops 1048576 | bytes 1614336 | tf_op jit(solution)/shard_map/transpose(jvp())/scatter-add | solution.py:48
  606.0 2.3 copy.72
  608.4 2.4 fusion.55
  610.8 248.3 %all-reduce.15.cloned.1.call-done = f32[64,2048]{1,0:T(8,128)} async-done(((f32[64,2048]{1,0:T(8,128)}), f32[64,2048]{1,0:T(8,128)}) %all-reduce.15.cloned.1.call-update) | async-done | bytes 524304 | tf_op jit(solution)/shard_map/psum | solution.py:119
  859.2 2.6 fusion.100
  862.6 1.7 fusion.34
  864.4 8.9 while.43
  864.4 4.4 fusion.176
  868.8 4.4 fusion.176
  875.3 1.7 fusion.36
  877.0 2.6 fusion.62
  879.6 1.9 fusion.99
  885.9 1.4 convolution_bitcast_fusion.2
  888.7 5.7 fusion.21
  894.4 3.3 copy-done.1
  897.7 2.5 fusion.95
  900.2 2.5 fusion.104
  903.9 88.0 %scatter_custom_fusion.2 = f32[64,2560]{0,1:T(8,128)S(1)} fusion(s32[16384]{0:T(1024)S(1)} %bitcast.240, f32[16384,64]{1,0:T(8,128)} %bitcast.227, f32[]{:T(128)} %constant.19.clone.1), kind=kCustom, calls=%fused_computation.85 | custom fusion | flops 1048576 | bytes 655872 | tf_op jit(solution)/shard_map/transpose(jvp())/scatter-add | solution.py:33
  991.9 2.2 fusion.103
  994.1 1.6 convolution_bitcast_fusion
  995.8 1.7 fusion.33
  997.5 1.9 collective-permute-start.4
  999.4 1.9 collective-permute-start.7
  1002.6 1.9 collective-permute-start.5
  1004.6 1.5 pad_add_fusion.2
  1006.6 1.5 pad_add_fusion
  1008.5 2.5 fusion.65
  1011.0 2.4 fusion.108
  1013.7 142.5 %all-reduce.17.cloned.1.call-done = (f32[64,128]{1,0:T(8,128)}, f32[64,64]{1,0:T(8,128)}, f32[64,128]{1,0:T(8,128)}, f32[64,64]{1,0:T(8,128)}, f32[64,64]{1,0:T(...) async-done(((f32[64,128]{1,0:T(8,128)}, f32[64,64]{1,0:T(8,128)}, f32[64,128]{1,0:T(8,128)}, f32[64,64]{1,0:T(8,128)}, f32[64,64]{1,0:T(8,128)}, ...) | async-done | bytes 164624 | tf_op jit(solution)/shard_map/psum | solution.py:207
  1156.4 3.7 scatter_fusion
  1161.2 56.1 %all-reduce.19.cloned.1.call-done = (f32[64,128]{1,0:T(8,128)}, f32[64,64]{1,0:T(8,128)}, f32[64,128]{1,0:T(8,128)}, f32[64,64]{1,0:T(8,128)}, f32[64,64]{1,0:T(...) async-done(((f32[64,128]{1,0:T(8,128)}, f32[64,64]{1,0:T(8,128)}, f32[64,128]{1,0:T(8,128)}, f32[64,64]{1,0:T(8,128)}, f32[64,64]{1,0:T(8,128)}, ...) | async-done | bytes 164624 | tf_op jit(solution)/shard_map/psum | solution.py:220
  1218.7 1.5 copy.79
  1220.7 1.4 copy.147
  1222.1 1.4 copy.148
  1223.5 1.4 copy.149
  (146 shorter events, 44.6 us)
Async XLA Ops:
  7.2 359.9 %copy-start = (f32[64,64]{1,0:T(8,128)S(1)}, f32[64,64]{1,0:T(8,128)}, u32[]{:S(2)}) copy-start(f32[64,64]{1,0:T(8,128)} %param.37) | copy-start | bytes 49156
  7.2 357.4 %all-reduce.13.cloned.1.call-start = ((), (), s32[]{:S(2)}) async-start(), calls=%async_computation | async-start | bytes 1048576 | tf_op jit(solution)/shard_map/psum | solution.py:119
  10.5 22.6 %collective-permute-start.3 = (f32[64,128]{1,0:T(8,128)S(1)}, f32[64,128]{1,0:T(8,128)S(1)}, u32[]{:S(2)}, u32[]{:S(2)}) collective-permute-start(f32[64,128]{1,0:T(8,128)S(1)} %get-tuple-element.226), channel_id=1, source_target_pairs={{1,0},{2,1},{3,2},{4,3},{5,4},{6,5},{7,6},{8,7},{9,8},{10,9},{11,1... | collective-permute-start | bytes 98312 | tf_op jit(solution)/shard_map/ppermute | solution.py:14
  11.8 21.3 %collective-permute-start.2 = (f32[64,128]{1,0:T(8,128)S(1)}, f32[64,128]{1,0:T(8,128)S(1)}, u32[]{:S(2)}, u32[]{:S(2)}) collective-permute-start(f32[64,128]{1,0:T(8,128)S(1)} %get-tuple-element.227), channel_id=1, source_target_pairs={{0,1},{1,2},{2,3},{3,4},{4,5},{5,6},{6,7},{7,8},{8,9},{9,10},{10,1... | collective-permute-start | bytes 98312 | tf_op jit(solution)/shard_map/ppermute | solution.py:14
  16.3 16.7 %collective-permute-start.1 = (f32[64,128]{1,0:T(8,128)S(1)}, f32[64,128]{1,0:T(8,128)S(1)}, u32[]{:S(2)}, u32[]{:S(2)}) collective-permute-start(f32[64,128]{1,0:T(8,128)S(1)} %get-tuple-element.228), channel_id=1, source_target_pairs={{32,0},{64,32},{96,64},{128,96},{160,128},{192,160},{224,192},{33,... | collective-permute-start | bytes 98312 | tf_op jit(solution)/shard_map/ppermute | solution.py:14
  18.3 14.7 %collective-permute-start = (f32[64,128]{1,0:T(8,128)S(1)}, f32[64,128]{1,0:T(8,128)S(1)}, u32[]{:S(2)}, u32[]{:S(2)}) collective-permute-start(f32[64,128]{1,0:T(8,128)S(1)} %get-tuple-element.229), channel_id=1, source_target_pairs={{0,32},{32,64},{64,96},{96,128},{128,160},{160,192},{192,224},{1,3... | collective-permute-start | bytes 98312 | tf_op jit(solution)/shard_map/ppermute | solution.py:14
  23.7 6.4 copy-start.24
  23.7 12.1 copy-start.23
  27.2 63.4 %copy-start.3 = (f32[64,2048]{0,1:T(8,128)}, f32[64,2048]{0,1:T(8,128)S(1)}, u32[]{:S(2)}) copy-start(f32[64,2048]{0,1:T(8,128)S(1)} %fusion.81) | copy-start | bytes 1572868
  33.1 0.8 copy-start.5
  90.6 4.9 copy-start.22
  90.6 7.0 copy-start.18
  90.6 7.6 copy-start.2
  90.6 9.0 copy-start.29
  90.6 9.8 copy-start.16
  96.8 0.8 copy-start.7
  98.8 0.8 copy-start.15
  100.3 8.3 copy-start.9
  100.4 8.2 copy-start.26
  100.4 8.3 copy-start.19
  100.4 264.2 %copy-start.21 = (f32[64,64]{1,0:T(8,128)S(1)}, f32[64,64]{1,0:T(8,128)}, u32[]{:S(2)}) copy-start(f32[64,64]{1,0:T(8,128)} %param.36) | copy-start | bytes 49156
  107.4 353.2 %copy-start.20 = (f32[64,64]{1,0:T(8,128)S(1)}, f32[64,64]{1,0:T(8,128)}, u32[]{:S(2)}) copy-start(f32[64,64]{1,0:T(8,128)} %param.38) | copy-start | bytes 49156
  108.3 750.8 %all-reduce.15.cloned.1.call-start = ((), (), s32[]{:S(2)}) async-start(), calls=%async_computation.1 | async-start | bytes 1048576 | tf_op jit(solution)/shard_map/psum | solution.py:119
  366.3 0.8 copy-start.17
  462.8 11.1 copy-start.28
  462.8 15.5 %copy-start.25 = (f32[64,64]{1,0:T(8,128)S(1)}, f32[64,64]{1,0:T(8,128)}, u32[]{:S(2)}) copy-start(f32[64,64]{1,0:T(8,128)} %param.40) | copy-start | bytes 49156
  473.9 8.3 copy-start.10
  608.4 547.8 %all-reduce.17.cloned.1.call-start = ((), (), s32[]{:S(2)}) async-start(), calls=%async_computation.2 | async-start | bytes 462848 | tf_op jit(solution)/shard_map/psum | solution.py:207
  861.8 0.8 copy-start.11
  864.3 15.3 %copy-start.30 = (f32[64,64]{1,0:T(8,128)S(1)}, f32[64,64]{1,0:T(8,128)}, u32[]{:S(2)}) copy-start(f32[64,64]{1,0:T(8,128)} %param.35) | copy-start | bytes 49156
  873.3 0.8 copy-start.12
  874.1 7.4 copy-start.8
  874.1 14.6 %copy-start.4 = (f32[64,2048]{0,1:T(8,128)S(1)}, f32[64,2048]{0,1:T(8,128)}, u32[]{:S(2)}) copy-start(f32[64,2048]{0,1:T(8,128)} %copy-done.3) | copy-start | bytes 1572868
  877.0 5.7 copy-start.13
  894.4 3.3 copy-start.1
  897.7 4.9 copy-start.14
  897.7 94.2 %copy-start.6 = (f32[64,2560]{1,0:T(8,128)S(1)}, f32[64,2560]{1,0:T(8,128)}, u32[]{:S(2)}) copy-start(f32[64,2560]{1,0:T(8,128)} %copy-done.5) | copy-start | bytes 1966084
  991.9 228.2 %copy-start.27 = (f32[64]{0:T(128)S(1)}, f32[64]{0:T(128)}, u32[]{:S(2)}) copy-start(f32[64]{0:T(128)} %get-tuple-element.239) | copy-start | bytes 772
  997.5 158.8 %collective-permute-start.4 = (f32[64,128]{1,0:T(8,128)S(1)}, f32[64,128]{1,0:T(8,128)S(1)}, u32[]{:S(2)}, u32[]{:S(2)}) collective-permute-start(f32[64,128]{1,0:T(8,128)S(1)} %get-tuple-element.222), channel_id=1, source_target_pairs={{32,0},{64,32},{96,64},{128,96},{160,128},{192,160},{224,192},{33,... | collective-permute-start | bytes 98312 | tf_op jit(solution)/shard_map/ppermute | solution.py:14
  999.4 156.8 %collective-permute-start.7 = (f32[64,128]{1,0:T(8,128)S(1)}, f32[64,128]{1,0:T(8,128)S(1)}, u32[]{:S(2)}, u32[]{:S(2)}) collective-permute-start(f32[64,128]{1,0:T(8,128)S(1)} %get-tuple-element.223), channel_id=1, source_target_pairs={{0,1},{1,2},{2,3},{3,4},{4,5},{5,6},{6,7},{7,8},{8,9},{9,10},{10,1... | collective-permute-start | bytes 98312 | tf_op jit(solution)/shard_map/ppermute | solution.py:14
  1001.3 154.9 %collective-permute-start.6 = (f32[64,128]{1,0:T(8,128)S(1)}, f32[64,128]{1,0:T(8,128)S(1)}, u32[]{:S(2)}, u32[]{:S(2)}) collective-permute-start(f32[64,128]{1,0:T(8,128)S(1)} %get-tuple-element.224), channel_id=1, source_target_pairs={{1,0},{2,1},{3,2},{4,3},{5,4},{6,5},{7,6},{8,7},{9,8},{10,9},{11,1... | collective-permute-start | bytes 98312 | tf_op jit(solution)/shard_map/ppermute | solution.py:14
  1002.6 153.6 %collective-permute-start.5 = (f32[64,128]{1,0:T(8,128)S(1)}, f32[64,128]{1,0:T(8,128)S(1)}, u32[]{:S(2)}, u32[]{:S(2)}) collective-permute-start(f32[64,128]{1,0:T(8,128)S(1)} %get-tuple-element.225), channel_id=1, source_target_pairs={{0,32},{32,64},{64,96},{96,128},{128,160},{160,192},{192,224},{1,3... | collective-permute-start | bytes 98312 | tf_op jit(solution)/shard_map/ppermute | solution.py:14
  1008.1 209.2 %all-reduce.19.cloned.1.call-start = ((), (), s32[]{:S(2)}) async-start(), calls=%async_computation.3 | async-start | bytes 462848 | tf_op jit(solution)/shard_map/psum | solution.py:220
Sparse Core Ops, SparseCore 0:
  108.4 256.1 all-reduce.12
  608.5 250.5 all-reduce.14
  1008.3 147.8 all-reduce.16
  1158.9 58.3 all-reduce.18
